TPU v7x, 32 devices: a whole 2x2x4 slice. The times are simulated.
32 devices in a mesh: tm: 16 (over z, x, core), rows: 2 (over y).
Axes of the slice: x: 2, y: 2, z: 4, core: 2. Of those that a mesh axis runs over, the one named last changes fastest.
Arguments:
- frames: bfloat16 [32, 16, 128, 128], P('tm', 'rows'), may hold values from -6 to 6
- conv_fine: bfloat16 [3, 3, 384, 128], replicated, may hold values from -0.109375 to 0.109375
- conv_down: bfloat16 [3, 384, 256], replicated, may hold values from -0.1875 to 0.1875
- conv_coarse: bfloat16 [3, 3, 768, 256], replicated, may hold values from -0.078125 to 0.078125
Outputs:
- coarse_out: bfloat16 [16, 8, 64, 256], P('tm', 'rows')
All inputs are finite; a program needn't handle non-finite values.
Results may differ from a plain program's by a relative error of at most 0.014.
Values may be sent and summed in bfloat16 or wider, within the bound.
No kernel may reach another device: no remote copies, remote signals or barrier semaphores. Data moves between devices by JAX's collectives and lax.ppermute only.
A program may use at most 64 MiB of HBM per device.

v0:
```python
import functools

import jax
import jax.numpy as jnp
from jax import lax
from jax.experimental import pallas as pl
from jax.experimental.pallas import tpu as pltpu
from jax.sharding import PartitionSpec as P


F32 = jnp.float32
BF16 = jnp.bfloat16


def moved(value, steps, hop):
    tm, rows = lax.axis_size("tm"), lax.axis_size("rows")
    pairs = [
        (t * rows + r, (t + steps) * rows + r + hop)
        for t in range(tm - steps)
        for r in range(rows)
        if 0 <= r + hop < rows
    ]
    return lax.ppermute(value, ("tm", "rows"), pairs)


def ring(value, steps):
    tm = lax.axis_size("tm")
    return lax.ppermute(value, "tm", [(t, (t + steps) % tm) for t in range(tm)])


def swapped(value, steps):
    tm = lax.axis_size("tm")
    pairs = [(t * 2 + r, (t + steps) * 2 + 1 - r) for t in range(tm - steps) for r in range(2)]
    return lax.ppermute(value, ("tm", "rows"), pairs)


def odd_ahead(value):
    tm = lax.axis_size("tm")
    pairs = [(t, t + 2) for t in range(1, tm - 2, 2)] + [(t, t) for t in range(0, tm, 2)]
    return lax.ppermute(value, "tm", pairs)


def even_ahead(value):
    tm, rows = lax.axis_size("tm"), lax.axis_size("rows")
    pairs = [(t, r, t + 2, r) for t in range(0, tm - 2, 2) for r in range(rows)]
    if tm % 4 == 0 and rows % 2 == 0:
        for r in range(rows):
            pairs += [(tm - 2, r, tm - 1, r), (tm - 1, r, tm - 3, r), (1, r, 0, r)]
            pairs += [(t, r, t - 4, r) for t in range(5, tm, 4)]
            pairs += [(t, r, t, r ^ 1) for t in range(3, tm - 1, 4)]
    return lax.ppermute(value, ("tm", "rows"), [(t * rows + r, u * rows + q) for t, r, u, q in pairs])


def paired(value):
    return lax.ppermute(value, "tm", [(t, t ^ 1) for t in range(lax.axis_size("tm"))])


def has_above():
    return lax.axis_index("rows") > 0


def has_below():
    return lax.axis_index("rows") < lax.axis_size("rows") - 1


def has_earlier(steps):
    return lax.axis_index("tm") >= steps


def pace_kernel(out):
    out[...] = jnp.zeros_like(out)


def edge_kernel(_, cells, out):
    width = out.shape[1]
    first = (1 - lax.axis_index("rows")) * (cells.shape[1] - width)
    out[...] = cells[:, pl.ds(first, width)]


def frame_rims(pace, frames):
    rows = frames.shape[1]
    if lax.axis_size("rows") == 2:
        sent = call(
            edge_kernel,
            jax.ShapeDtypeStruct((frames.shape[0], 2, *frames.shape[2:]), BF16),
            [],
            0,
            (pace, frames),
        )
        return [(both, both) for both in (swapped(sent, 0), swapped(sent, 1))]
    head, tail = frames[:, :2], frames[:, rows - 1 :]
    return [(moved(tail, steps, 1), moved(head, steps, -1)) for steps in (0, 1)]


def column_shift(value, cols, steps):
    size = value.shape[0]
    column = lax.broadcasted_iota(jnp.int32, value.shape, 0) % cols
    edge = 0 if steps > 0 else cols - 1
    return jnp.where(column == edge, 0.0, pltpu.roll(value, steps % size, 0))


def shifted_columns(flat, cols):
    wide = flat.astype(F32)
    return column_shift(wide, cols, 1).astype(BF16), column_shift(wide, cols, -1).astype(BF16)


def tap_matrix(weight, first_tap, row_taps, e, channels):
    zero = jnp.zeros((channels, channels), BF16)

    def pick(tap, b):
        return weight[tap, b, e * channels : (e + 1) * channels] if 0 <= tap <= 2 else zero

    return jnp.concatenate(
        [
            jnp.concatenate([pick(first_tap + f, b), pick(first_tap + f - 1, b)], axis=1)
            for f in range(2)
            for b in row_taps
        ],
        axis=0,
    )


def fine_rows(row, outs, row_taps, weight, first_tap):
    channels = weight.shape[-1]
    some = next(x for f in range(2) for r in outs for b in row_taps if (x := row(f, r - 1 + b)) is not None)
    cols = some.shape[0]
    zero = jnp.zeros((cols, channels), BF16)

    def cell(f, i):
        found = row(f, i)
        return zero if found is None else found

    left = jnp.concatenate(
        [
            jnp.concatenate([cell(f, r - 1 + b) for f in range(2) for b in row_taps], axis=1)
            for r in outs
        ],
        axis=0,
    )
    sums = [
        jnp.dot(
            left, tap_matrix(weight, first_tap, row_taps, e, channels), preferred_element_type=F32
        )
        for e in range(3)
    ]
    return sums[1] + column_shift(sums[0], cols, 1) + column_shift(sums[2], cols, -1)


def previous_rows(row, outs, weight):
    channels = weight.shape[-1]
    cols = next(x for r in outs if (x := row(1, r)) is not None).shape[0]
    zero = jnp.zeros((cols, channels), BF16)
    none = jnp.zeros((channels, channels), BF16)

    def cells(taps):
        lines = [
            jnp.concatenate([zero if (x := row(f, r - 1 + b)) is None else x for f, b in taps], axis=1)
            for r in outs
        ]
        return jnp.concatenate(lines, axis=0)

    def part(tap, b, e):
        return weight[tap, b, e * channels : (e + 1) * channels]

    def pair(left, right):
        return jnp.concatenate([left, right], axis=1)

    dot = functools.partial(jnp.dot, preferred_element_type=F32)
    near = cells([(1, 0), (1, 1), (1, 2), (0, 2)])
    sums = []
    for e in range(3):
        right = [pair(part(1, b, e), part(0, b, e)) for b in range(3)] + [pair(part(0, 2, e), none)]
        sums.append(dot(near, jnp.concatenate(right, axis=0)))
    far = cells([(0, 0), (0, 1)])
    both = dot(far, jnp.concatenate([pair(part(0, b, 0), part(0, b, 1)) for b in range(2)], axis=0))
    last = dot(far, jnp.concatenate([part(0, b, 2) for b in range(2)], axis=0))
    old = (both[:, :channels], both[:, channels:], last)
    first = [x[:, :channels] + y for x, y in zip(sums, old)]
    second = [x[:, channels:] for x in sums]
    return pair(*(
        x[1] + column_shift(x[0], cols, 1) + column_shift(x[2], cols, -1) for x in (first, second)
    ))


def chunks_of(count):
    size = next(c for c in (4, 3, 2, 1) if count % c == 0)
    return [range(i, i + size) for i in range(0, count, size)]


def fine_own_kernel(frames, weight, out):
    _, rows, cols, _ = frames.shape

    def row(f, i):
        return frames[f, i] if 0 <= i < rows else None

    for outs in chunks_of(rows + 1):
        out[outs[0] * cols : (outs[-1] + 1) * cols] = fine_rows(row, outs, range(3), weight, 2)


def halo_row(above, below, rows):
    def row(f, i):
        if i == -1:
            cells, have = above[f, above.shape[1] - 1], has_above()
        elif i >= rows:
            cells, have = below[f, i - rows], has_below()
        else:
            return None
        return jnp.where(have, cells, jnp.zeros_like(cells))

    return row


def halo_sum(above, below, weight, first_tap, rows):
    row = halo_row(above, below, rows)
    return jnp.concatenate(
        [
            fine_rows(row, [0], [0], weight, first_tap),
            fine_rows(row, [rows - 1, rows], [1, 2], weight, first_tap),
        ],
        axis=0,
    )


def fine_halo_kernel(above, below, weight, out, *, rows):
    out[...] = halo_sum(above, below, weight, 2, rows)


def silu(v):
    return v / (1.0 + jnp.exp(-v))


def fine_rest_kernel(frames, weight, own, halo, out):
    _, rows, cols, _ = frames.shape

    def row(f, i):
        return frames[f, i] if 0 <= i < rows else None

    for outs in chunks_of(rows + 1):
        total = jnp.where(has_earlier(1), previous_rows(row, outs, weight), 0.0)
        for i, r in enumerate(outs):
            line = total[i * cols : (i + 1) * cols] + own[r * cols : (r + 1) * cols]
            for k, halo_r in enumerate((0, rows - 1, rows)):
                if r == halo_r:
                    line = line + halo[k * cols : (k + 1) * cols]
            out[r * cols : (r + 1) * cols] = line


def pool(sums):
    channels = sums.shape[1] // 2
    fine = silu(sums).astype(BF16).astype(F32)
    return ((fine[:, :channels] + fine[:, channels:]) * 0.5).astype(BF16).astype(F32)


def down_taps(pooled, half_cols):
    return [
        jnp.concatenate(
            [pooled[i, pl.ds(e, half_cols, stride=2), :].astype(BF16) for e in range(3)], axis=1
        )
        for i in range(pooled.shape[0])
    ]


def put_pooled(pooled, lines):
    cols = lines[0].shape[0]
    pad = pooled.shape[1] - cols
    pooled[:, cols:] = jnp.zeros((pooled.shape[0], pad, pooled.shape[2]), F32)
    for i, line in enumerate(lines):
        pooled[i, :cols] = line


def reduced_rows(lines, firsts, half_cols, down, pooled):
    put_pooled(pooled, lines)
    taps = down_taps(pooled, half_cols)
    left = [jnp.concatenate(taps[i : i + 3], axis=1) for i in firsts]
    right = down[...].reshape(-1, down.shape[-1])
    rows = jnp.dot(jnp.concatenate(left, axis=0), right, preferred_element_type=F32)
    return rows.astype(BF16).reshape(len(firsts), half_cols, -1)


def inner_kernel(sums, down, out, pooled):
    count, half_cols, _ = out.shape
    cols = 2 * half_cols
    size = 2 * count + 1
    two = lax.axis_size("rows") == 2
    start = 2 * lax.axis_index("rows") if two else 2
    mean = pool(sums[pl.ds(pl.multiple_of(start * cols, cols), size * cols), :])
    lines = [mean[k * cols : (k + 1) * cols] for k in range(size)]
    if two:
        lines[-1] = jnp.where(has_below(), lines[-1], 0.0)
    out[...] = reduced_rows(lines, range(0, 2 * count, 2), half_cols, down, pooled)


def one_halo_sum(rims, weight):
    cols, channels = rims.shape[2:]
    up = has_above()
    zero = jnp.zeros((cols, channels), BF16)
    left = jnp.concatenate(
        [
            jnp.concatenate(
                [x for f in range(2) for x in (jnp.where(up, rims[f, 1], zero), jnp.where(up, zero, rims[f, 0]))],
                axis=1,
            ),
            jnp.concatenate([jnp.where(up, zero, rims[f, k]) for f in range(2) for k in range(2)], axis=1),
        ],
        axis=0,
    )
    b = 1 - lax.axis_index("rows")
    x = [
        jnp.dot(left, tap_matrix(weight, 0, (b, b + 1), e, channels), preferred_element_type=F32)
        for e in range(3)
    ]
    added = x[1] + column_shift(x[0], cols, 1) + column_shift(x[2], cols, -1)
    none = jnp.zeros((cols, added.shape[1]), F32)
    below = jnp.concatenate([none, added], axis=0)
    return jnp.where(up, jnp.concatenate([added[:cols], none, none], axis=0), below)


def reduce_kernel(above, below, weight, sums, inner, down, out, pooled):
    cols = above.shape[2]
    rows = sums.shape[0] // cols - 1
    half = rows // 2
    if lax.axis_size("rows") == 2:
        strip = lax.axis_index("rows")
        begin = pl.multiple_of((rows - 2) * (1 - strip) * cols, cols)
        mean = pool(sums[pl.ds(begin, 3 * cols), :] + one_halo_sum(above, weight))
        lines = [mean[k * cols : (k + 1) * cols] for k in range(3)]
        end = reduced_rows(lines, (0,), cols // 2, down, pooled)
        out[0, pl.ds(strip, half - 1)] = inner[...]
        out[0, (half - 1) * (1 - strip)] = end[0]
        return
    added = halo_sum(above, below, weight, 0, rows)
    lines = []
    for r in (0, 1, 2, rows - 2, rows - 1, rows):
        line = sums[r * cols : (r + 1) * cols]
        for k, halo_r in enumerate((0, rows - 1, rows)):
            if r == halo_r:
                line = line + added[k * cols : (k + 1) * cols]
        line = pool(line)
        lines.append(jnp.where(has_below(), line, 0.0) if r == rows else line)
    ends = reduced_rows(lines, (0, 3), cols // 2, down, pooled)
    out[0, 0] = ends[0]
    out[0, 1 : half - 1] = inner[...]
    out[0, half - 1] = ends[1]


def column_taps(flat, cols):
    left, right = shifted_columns(flat, cols)
    return jnp.concatenate([left, flat, right], axis=1)


def coarse_sums(field, weight, a, sides):
    _, rows, cols, channels = field.shape
    body = column_taps(field.reshape(rows * cols, channels), cols)
    zero = jnp.zeros_like(body[:cols])
    tall = jnp.concatenate([zero, body, zero], axis=0)
    dot = functools.partial(jnp.dot, preferred_element_type=F32)
    total = sum(dot(tall[b * cols : (b + rows) * cols], weight[a, b]) for b in range(3))
    head, tail = body[:cols], body[(rows - 1) * cols :]
    if sides == 1:
        return total, [dot(jnp.where(has_above(), head, tail), weight[a, 2 * lax.axis_index("rows")])]
    return total, [dot(tail, weight[a, 0]), dot(head, weight[a, 2])]


def coarse_first_kernel(field, weight, body, ends):
    total, parts = coarse_sums(field[...], weight, 2, ends.shape[0])
    body[...] = total
    for side, part in enumerate(parts):
        ends[side] = part


def earlier_sums(field_1, odd_field, even_field, weight, sides):
    one = field_1[...]
    one = jnp.where(has_earlier(1), one, jnp.zeros_like(one))
    two = jnp.where(lax.axis_index("tm") % 2 == 1, odd_field[...], even_field[...])
    two = jnp.where(has_earlier(2), two, jnp.zeros_like(two))
    total_1, ends_1 = coarse_sums(one, weight, 1, sides)
    total_2, ends_2 = coarse_sums(two, weight, 0, sides)
    return total_1 + total_2, [x + y for x, y in zip(ends_1, ends_2)]


def coarse_ends_kernel(field_1, odd_field, even_field, weight, ends, out):
    _, parts = earlier_sums(field_1, odd_field, even_field, weight, ends.shape[0])
    for side, part in enumerate(parts):
        out[side] = (ends[side] + part).astype(BF16)


def end_starts(rows, sides):
    return [(rows - 1) * (1 - lax.axis_index("rows"))] if sides == 1 else [0, rows - 1]


def coarse_body_kernel(field_1, odd_field, even_field, weight, body, out, ends, sums):
    _, rows, cols, _ = out.shape
    total, _ = earlier_sums(field_1, odd_field, even_field, weight, ends.shape[0])
    sums[...] = body[...] + total
    out[...] = silu(sums[...]).astype(BF16).reshape(out.shape)
    for side, start in enumerate(end_starts(rows, ends.shape[0])):
        ends[side] = sums[pl.ds(pl.multiple_of(start * cols, cols), cols), :]


def finish_kernel(ends, added, _, out, lines, sem):
    rows = out.shape[1]
    copies = []
    for side, start in enumerate(end_starts(rows, ends.shape[0])):
        total = ends[side] + added[side].astype(F32)
        lines[side] = silu(total).astype(BF16)
        copies.append(
            pltpu.make_async_copy(lines.at[side], out.at[0, start], sem.at[side])
        )
        copies[-1].start()
    for copy in copies:
        copy.wait()


def call(kernel, out_shape, scratch, flops, args, in_place=False):
    size = sum(a.size * a.dtype.itemsize for a in args)
    vmem = pl.BlockSpec(memory_space=pltpu.VMEM)
    last = pl.BlockSpec(memory_space=pl.ANY) if in_place else vmem
    return pl.pallas_call(
        kernel,
        out_shape=out_shape,
        in_specs=[vmem] * (len(args) - 1) + [last] if args else [],
        out_specs=last if in_place else jax.tree.map(lambda _: vmem, out_shape),
        input_output_aliases={len(args) - 1: 0} if in_place else {},
        scratch_shapes=scratch,
        cost_estimate=pl.CostEstimate(flops=flops, bytes_accessed=size, transcendentals=0),
        compiler_params=pltpu.CompilerParams(vmem_limit_bytes=20 * 1024 * 1024),
    )(*args)


def local(frames, conv_fine, conv_down, conv_coarse):
    _, rows, cols, channels = frames.shape
    wide = conv_down.shape[-1]
    strips, times = lax.axis_size("rows"), lax.axis_size("tm")
    pace = call(pace_kernel, jax.ShapeDtypeStruct((8, 128), F32), [], 4 * 10**9, ())

    earlier = ring(frames, 1)
    (above, below), (above_1, below_1) = frame_rims(pace, frames)
    size = (rows + 1) * cols
    pair = jax.ShapeDtypeStruct((size, 2 * channels), F32)
    flops = 2 * size * 18 * channels * 2 * channels
    own = call(fine_own_kernel, pair, [], flops, (frames, conv_fine))
    halo = call(
        functools.partial(fine_halo_kernel, rows=rows),
        jax.ShapeDtypeStruct((3 * cols, 2 * channels), F32),
        [],
        flops // 3,
        (above, below, conv_fine),
    )
    half_rows, half_cols = rows // 2, cols // 2
    shape = jax.ShapeDtypeStruct((1, half_rows, half_cols, wide), BF16)
    fine_sums = call(fine_rest_kernel, pair, [], flops, (earlier, conv_fine, own, halo))
    inner = call(
        inner_kernel,
        jax.ShapeDtypeStruct((half_rows - (1 if strips == 2 else 2), half_cols, wide), BF16),
        [pltpu.VMEM((rows - (1 if strips == 2 else 3), cols + 8, channels), F32)],
        flops // 4,
        (fine_sums, conv_down),
    )
    above_1, below_1, fine_sums, inner = lax.optimization_barrier(
        (above_1, below_1, fine_sums, inner)
    )
    field = call(
        reduce_kernel,
        shape,
        [pltpu.VMEM((3 if strips == 2 else 6, cols + 8, channels), F32)],
        flops // 3,
        (above_1, below_1, conv_fine, fine_sums, inner, conv_down),
    )
    sides = 1 if strips == 2 else 2
    sums = jax.ShapeDtypeStruct((half_rows * half_cols, wide), F32)
    pairs = jax.ShapeDtypeStruct((sides, half_cols, wide), F32)
    flops = 2 * half_rows * half_cols * 9 * wide * wide
    odd_field = odd_ahead(field)
    even_field = even_ahead(field)
    body, ends = call(coarse_first_kernel, (sums, pairs), [], flops, (field, conv_coarse))
    odd_field, body, ends = lax.optimization_barrier((odd_field, body, ends))
    field_1 = paired(odd_field) if times % 2 == 0 else ring(field, 1)
    sent = call(
        coarse_ends_kernel,
        jax.ShapeDtypeStruct(pairs.shape, BF16),
        [],
        flops // 4,
        (field_1, odd_field, even_field, conv_coarse, ends),
    )
    if sides == 1:
        added = swapped(sent, 0)
    else:
        added = jnp.concatenate([moved(sent[:1], 0, 1), moved(sent[1:], 0, -1)], axis=0)
    out, end_sums = call(
        coarse_body_kernel,
        (shape, pairs),
        [pltpu.VMEM(sums.shape, F32)],
        flops,
        (field_1, odd_field, even_field, conv_coarse, body),
    )
    return call(
        finish_kernel,
        shape,
        [pltpu.VMEM((sides, half_cols, wide), BF16), pltpu.SemaphoreType.DMA((sides,))],
        flops // 16,
        (end_sums, added, out),
        in_place=True,
    )


def solution(mesh):
    placed = (P("tm", "rows", None, None), P(), P(), P())
    return jax.shard_map(local, mesh=mesh, in_specs=placed, out_specs=P("tm", "rows", None, None), check_vma=False)
```

profile of v0, /device:TPU:16, one launch (start us, length us, event | category | flops | bytes accessed | tf_op | source)
XLA Modules:
  0.0 24.3 jit_solution(7107747464431544156)
XLA Ops:
  0.0 0.0 copy-start.3
  0.0 0.0 copy-start.2
  0.0 0.0 collective-permute-start.1
  0.0 1.0 %copy-done.3 = bf16[2,8,128,128]{3,2,1,0:T(8,128)(2,1)S(1)} copy-done((bf16[2,8,128,128]{3,2,1,0:T(8,128)(2,1)S(1)}, bf16[2,8,128,128]{3,2,1,0:T(8,128)(2,1)}, u32[]{:S(2)}) %copy-start.3) | copy-done | bytes 524312
  1.1 1.6 %collective-permute-start.2 = (bf16[2,2,128,128]{3,2,1,0:T(8,128)(2,1)S(1)}, bf16[2,2,128,128]{3,2,1,0:T(8,128)(2,1)S(1)}, u32[]{:S(2)}, u32[]{:S(2)}) collective-permute-start(bf16[2,2,128,128]{3,2,1,0:T(8,128)(2,1)S(1)} %shard_map.47), channel_id=1, source_target_pairs={{0,1},{1,0},{2,3},{3,2},{4,5},{5,4},{6,7},{7,6},{8,9},{9,8},{10,11... | collective-permute-start | bytes 393224 | tf_op jit(solution)/shard_map/ppermute | solution.py:34
  2.6 2.3 %collective-permute-start = (bf16[2,2,128,128]{3,2,1,0:T(8,128)(2,1)S(1)}, bf16[2,2,128,128]{3,2,1,0:T(8,128)(2,1)S(1)}, u32[]{:S(2)}, u32[]{:S(2)}) collective-permute-start(bf16[2,2,128,128]{3,2,1,0:T(8,128)(2,1)S(1)} %shard_map.47), channel_id=1, source_target_pairs={{0,3},{1,2},{2,5},{3,4},{4,7},{5,6},{6,9},{7,8},{8,11},{9,10},{10,... | collective-permute-start | bytes 393224 | tf_op jit(solution)/shard_map/ppermute | solution.py:34
  5.0 0.0 copy-done.2
  5.0 1.5 %shard_map.48.own = f32[1152,256]{1,0:T(8,128)S(1)} custom-call(bf16[2,8,128,128]{3,2,1,0:T(8,128)(2,1)S(1)} %copy-done.3, bf16[3,3,384,128]{3,2,1,0:T(8,128)(2,1)S(1)} %copy-done.2), custom_call_target="tpu_custom_call" | custom-call | flops 1358954496 | bytes 1409024 | tf_op jit(solution)/shard_map/pallas_call | solution.py:418
  6.5 0.6 %collective-permute-done.2.above.below = bf16[2,2,128,128]{3,2,1,0:T(8,128)(2,1)S(1)} collective-permute-done((bf16[2,2,128,128]{3,2,1,0:T(8,128)(2,1)S(1)}, bf16[2,2,128,128]{3,2,1,0:T(8,128)(2,1)S(1)}, u32[]{:S(2)}, u32[]{:S(2)}) %collective-permute-start.2) | collective-permute-done | bytes 131104 | tf_op jit(solution)/shard_map/ppermute | solution.py:34
  7.1 0.4 %shard_map.49.halo = f32[384,256]{1,0:T(8,128)S(1)} custom-call(bf16[2,2,128,128]{3,2,1,0:T(8,128)(2,1)S(1)} %collective-permute-done.2.above.below, bf16[2,2,128,128]{3,2,1,0:T(8,128)(2,1)S(1)} %collective-permute-done.2.above.below, bf16[3,3,384,128]{3,2,1,0:T(8,128)(2,1)S(1)} %copy-done.2), custom_call_target="tpu_custom_call" | custom-call | flops 452984832 | bytes 1146880 | tf_op jit(solution)/shard_map/pallas_call | solution.py:418
  7.5 0.0 copy-start.1
  7.5 2.2 %collective-permute-done.1.frames = bf16[2,8,128,128]{3,2,1,0:T(8,128)(2,1)S(1)} collective-permute-done((bf16[2,8,128,128]{3,2,1,0:T(8,128)(2,1)}, bf16[2,8,128,128]{3,2,1,0:T(8,128)(2,1)S(1)}, u32[]{:S(2)}, u32[]{:S(2)}) %collective-permute-start.1) | collective-permute-done | bytes 524320 | tf_op jit(solution)/shard_map/ppermute | solution.py:28
  9.7 1.4 %shard_map.50.sums = f32[1152,256]{1,0:T(8,128)S(1)} custom-call(bf16[2,8,128,128]{3,2,1,0:T(8,128)(2,1)S(1)} %collective-permute-done.1.frames, bf16[3,3,384,128]{3,2,1,0:T(8,128)(2,1)S(1)} %copy-done.2, f32[1152,256]{1,0:T(8,128)S(1)} %shard_map.48.own, f32[384,256]{1,0:T(8,128)S(1)} %shard_map.49.halo), custom_call_target="tpu_custom_call" | custom-call | flops 1358954496 | bytes 2981888 | tf_op jit(solution)/shard_map/pallas_call | solution.py:418
  11.1 0.0 copy-done.1
  11.1 0.0 copy-start
  11.2 0.6 %shard_map.51.inner = bf16[3,64,256]{2,1,0:T(8,128)(2,1)S(1)} custom-call(f32[1152,256]{1,0:T(8,128)S(1)} %shard_map.50.sums, bf16[3,384,256]{2,1,0:T(8,128)(2,1)S(1)} %copy-done.1), custom_call_target="tpu_custom_call" | custom-call | flops 339738624 | bytes 1769472 | tf_op jit(solution)/shard_map/pallas_call | solution.py:418
  11.7 0.4 %collective-permute-done.above.below = bf16[2,2,128,128]{3,2,1,0:T(8,128)(2,1)S(1)} collective-permute-done((bf16[2,2,128,128]{3,2,1,0:T(8,128)(2,1)S(1)}, bf16[2,2,128,128]{3,2,1,0:T(8,128)(2,1)S(1)}, u32[]{:S(2)}, u32[]{:S(2)}) %collective-permute-start) | collective-permute-done | bytes 131104 | tf_op jit(solution)/shard_map/ppermute | solution.py:34
  12.1 0.7 %shard_map.52.field = bf16[1,4,64,256]{3,2,1,0:T(8,128)(2,1)S(1)} custom-call(bf16[2,2,128,128]{3,2,1,0:T(8,128)(2,1)S(1)} %collective-permute-done.above.below, bf16[2,2,128,128]{3,2,1,0:T(8,128)(2,1)S(1)} %collective-permute-done.above.below, bf16[3,3,384,128]{3,2,1,0:T(8,128)(2,1)S(1)} %copy-done.2, f32[1152,256]{1,0:T(8,128)S(1)} %shard_map.50.sums, ...), custom_call_target="tpu_custom_call" | custom-call | flops 452984832 | bytes 3014656 | tf_op jit(solution)/shard_map/pallas_call | solution.py:418
  12.8 0.7 %collective-permute-start.3 = (bf16[1,4,64,256]{3,2,1,0:T(8,128)(2,1)S(1)}, bf16[1,4,64,256]{3,2,1,0:T(8,128)(2,1)S(1)}, u32[]{:S(2)}, u32[]{:S(2)}) collective-permute-start(bf16[1,4,64,256]{3,2,1,0:T(8,128)(2,1)S(1)} %shard_map.52.field), channel_id=1, source_target_pairs={{2,6},{6,10},{10,14},{14,18},{18,22},{22,26},{26,30},{0,0},{4,4},{... | collective-permute-start | bytes 393224 | tf_op jit(solution)/shard_map/ppermute | solution.py:40
  13.5 0.7 %collective-permute-start.5 = (bf16[1,4,64,256]{3,2,1,0:T(8,128)(2,1)S(1)}, bf16[1,4,64,256]{3,2,1,0:T(8,128)(2,1)S(1)}, u32[]{:S(2)}, u32[]{:S(2)}) collective-permute-start(bf16[1,4,64,256]{3,2,1,0:T(8,128)(2,1)S(1)} %shard_map.52.field), channel_id=1, source_target_pairs={{0,4},{1,5},{4,8},{5,9},{8,12},{9,13},{12,16},{13,17},{16,20},{17,... | collective-permute-start | bytes 393224 | tf_op jit(solution)/shard_map/ppermute | solution.py:51
  14.2 0.0 copy-done
  14.2 0.5 %shard_map.53 = (f32[256,256]{1,0:T(8,128)S(1)}, f32[1,64,256]{2,1,0:T(8,128)S(1)}) custom-call(bf16[1,4,64,256]{3,2,1,0:T(8,128)(2,1)S(1)} %shard_map.52.field, bf16[3,3,768,256]{3,2,1,0:T(8,128)(2,1)S(1)} %copy-done), custom_call_target="tpu_custom_call" | custom-call | flops 301989888 | bytes 3670016 | tf_op jit(solution)/shard_map/pallas_call | solution.py:418
  14.7 0.0 collective-permute-done.3.odd_field
  14.7 2.8 %collective-permute-start.4 = (bf16[1,4,64,256]{3,2,1,0:T(8,128)(2,1)S(1)}, bf16[1,4,64,256]{3,2,1,0:T(8,128)(2,1)S(1)}, u32[]{:S(2)}, u32[]{:S(2)}) collective-permute-start(bf16[1,4,64,256]{3,2,1,0:T(8,128)(2,1)S(1)} %collective-permute-done.3.odd_field), channel_id=1, source_target_pairs={{0,2},{2,0},{4,6},{6,4},{8,10},{10,8},{12,14},{14,12},{16,18},{18,... | collective-permute-start | bytes 393224 | tf_op jit(solution)/shard_map/ppermute | solution.py:55
  17.5 1.9 %collective-permute-done.5.even_field = bf16[1,4,64,256]{3,2,1,0:T(8,128)(2,1)S(1)} collective-permute-done((bf16[1,4,64,256]{3,2,1,0:T(8,128)(2,1)S(1)}, bf16[1,4,64,256]{3,2,1,0:T(8,128)(2,1)S(1)}, u32[]{:S(2)}, u32[]{:S(2)}) %collective-permute-start.5) | collective-permute-done | bytes 131104 | tf_op jit(solution)/shard_map/ppermute | solution.py:51
  19.4 0.0 collective-permute-done.4.field_1
  19.4 0.2 %shard_map.55 = bf16[1,64,256]{2,1,0:T(8,128)(2,1)S(1)} custom-call(bf16[1,4,64,256]{3,2,1,0:T(8,128)(2,1)S(1)} %collective-permute-done.4.field_1, bf16[1,4,64,256]{3,2,1,0:T(8,128)(2,1)S(1)} %collective-permute-done.3.odd_field, bf16[1,4,64,256]{3,2,1,0:T(8,128)(2,1)S(1)} %collective-permute-done.5.even_field, bf16[3,3,768,256]{3,2,1,0:T(8,128)(2,1)S(1)} %copy-done, ...), custom_call_target="tpu_custom_call" | custom-call | flops 75497472 | bytes 3997696 | tf_op jit(solution)/shard_map/pallas_call | solution.py:418
  19.7 1.2 %collective-permute-start.6 = (bf16[1,64,256]{2,1,0:T(8,128)(2,1)S(1)}, bf16[1,64,256]{2,1,0:T(8,128)(2,1)S(1)}, u32[]{:S(2)}, u32[]{:S(2)}) collective-permute-start(bf16[1,64,256]{2,1,0:T(8,128)(2,1)S(1)} %shard_map.55), channel_id=1, source_target_pairs={{0,1},{1,0},{2,3},{3,2},{4,5},{5,4},{6,7},{7,6},{8,9},{9,8},{10,11... | collective-permute-start | bytes 98312 | tf_op jit(solution)/shard_map/ppermute | solution.py:34
  20.9 1.5 %shard_map.54 = (bf16[1,4,64,256]{3,2,1,0:T(8,128)(2,1)}, f32[1,64,256]{2,1,0:T(8,128)S(1)}) custom-call(bf16[1,4,64,256]{3,2,1,0:T(8,128)(2,1)S(1)} %collective-permute-done.4.field_1, bf16[1,4,64,256]{3,2,1,0:T(8,128)(2,1)S(1)} %collective-permute-done.3.odd_field, bf16[1,4,64,256]{3,2,1,0:T(8,128)(2,1)S(1)} %collective-permute-done.5.even_field, ...), custom_call_target="tpu_custom_call" | custom-call | flops 301989888 | bytes 4194304 | tf_op jit(solution)/shard_map/pallas_call | solution.py:418
  22.4 1.3 %collective-permute-done.6.added = bf16[1,64,256]{2,1,0:T(8,128)(2,1)S(1)} collective-permute-done((bf16[1,64,256]{2,1,0:T(8,128)(2,1)S(1)}, bf16[1,64,256]{2,1,0:T(8,128)(2,1)S(1)}, u32[]{:S(2)}, u32[]{:S(2)}) %collective-permute-start.6) | collective-permute-done | bytes 32800 | tf_op jit(solution)/shard_map/ppermute | solution.py:34
  23.7 0.7 %shard_map.56 = bf16[1,4,64,256]{3,2,1,0:T(8,128)(2,1)} custom-call(f32[1,64,256]{2,1,0:T(8,128)S(1)} %get-tuple-element.24.ends, bf16[1,64,256]{2,1,0:T(8,128)(2,1)S(1)} %collective-permute-done.6.added, bf16[1,4,64,256]{3,2,1,0:T(8,128)(2,1)} %get-tuple-element.26._), custom_call_target="tpu_custom_call", output_to_operand_aliasing={{}: (2, {})} | custom-call | flops 18874368 | bytes 229376 | tf_op jit(solution)/shard_map/pallas_call | solution.py:418
  (2 shorter events, 0.0 us)
Async XLA Ops:
  0.0 1.0 %copy-start.3 = (bf16[2,8,128,128]{3,2,1,0:T(8,128)(2,1)S(1)}, bf16[2,8,128,128]{3,2,1,0:T(8,128)(2,1)}, u32[]{:S(2)}) copy-start(bf16[2,8,128,128]{3,2,1,0:T(8,128)(2,1)} %frames.1) | copy-start | bytes 1572868
  0.0 4.9 %copy-start.2 = (bf16[3,3,384,128]{3,2,1,0:T(8,128)(2,1)S(1)}, bf16[3,3,384,128]{3,2,1,0:T(8,128)(2,1)}, u32[]{:S(2)}) copy-start(bf16[3,3,384,128]{3,2,1,0:T(8,128)(2,1)} %weight.10) | copy-start | bytes 2654212
  0.0 9.7 %collective-permute-start.1 = (bf16[2,8,128,128]{3,2,1,0:T(8,128)(2,1)}, bf16[2,8,128,128]{3,2,1,0:T(8,128)(2,1)S(1)}, u32[]{:S(2)}, u32[]{:S(2)}) collective-permute-start(bf16[2,8,128,128]{3,2,1,0:T(8,128)(2,1)} %frames.1), channel_id=1, source_target_pairs={{0,2},{2,4},{4,6},{6,8},{8,10},{10,12},{12,14},{14,16},{16,18},{18... | collective-permute-start | bytes 1572872 | tf_op jit(solution)/shard_map/ppermute | solution.py:28
  1.1 6.0 %collective-permute-start.2 = (bf16[2,2,128,128]{3,2,1,0:T(8,128)(2,1)S(1)}, bf16[2,2,128,128]{3,2,1,0:T(8,128)(2,1)S(1)}, u32[]{:S(2)}, u32[]{:S(2)}) collective-permute-start(bf16[2,2,128,128]{3,2,1,0:T(8,128)(2,1)S(1)} %shard_map.47), channel_id=1, source_target_pairs={{0,1},{1,0},{2,3},{3,2},{4,5},{5,4},{6,7},{7,6},{8,9},{9,8},{10,11... | collective-permute-start | bytes 393224 | tf_op jit(solution)/shard_map/ppermute | solution.py:34
  2.6 9.4 %collective-permute-start = (bf16[2,2,128,128]{3,2,1,0:T(8,128)(2,1)S(1)}, bf16[2,2,128,128]{3,2,1,0:T(8,128)(2,1)S(1)}, u32[]{:S(2)}, u32[]{:S(2)}) collective-permute-start(bf16[2,2,128,128]{3,2,1,0:T(8,128)(2,1)S(1)} %shard_map.47), channel_id=1, source_target_pairs={{0,3},{1,2},{2,5},{3,4},{4,7},{5,6},{6,9},{7,8},{8,11},{9,10},{10,... | collective-permute-start | bytes 393224 | tf_op jit(solution)/shard_map/ppermute | solution.py:34
  7.5 3.6 %copy-start.1 = (bf16[3,384,256]{2,1,0:T(8,128)(2,1)S(1)}, bf16[3,384,256]{2,1,0:T(8,128)(2,1)}, u32[]{:S(2)}) copy-start(bf16[3,384,256]{2,1,0:T(8,128)(2,1)} %down.3) | copy-start | bytes 1769476
  11.1 3.0 %copy-start = (bf16[3,3,768,256]{3,2,1,0:T(8,128)(2,1)S(1)}, bf16[3,3,768,256]{3,2,1,0:T(8,128)(2,1)}, u32[]{:S(2)}) copy-start(bf16[3,3,768,256]{3,2,1,0:T(8,128)(2,1)} %weight.13) | copy-start | bytes 10616836
  12.8 1.9 %collective-permute-start.3 = (bf16[1,4,64,256]{3,2,1,0:T(8,128)(2,1)S(1)}, bf16[1,4,64,256]{3,2,1,0:T(8,128)(2,1)S(1)}, u32[]{:S(2)}, u32[]{:S(2)}) collective-permute-start(bf16[1,4,64,256]{3,2,1,0:T(8,128)(2,1)S(1)} %shard_map.52.field), channel_id=1, source_target_pairs={{2,6},{6,10},{10,14},{14,18},{18,22},{22,26},{26,30},{0,0},{4,4},{... | collective-permute-start | bytes 393224 | tf_op jit(solution)/shard_map/ppermute | solution.py:40
  13.5 5.9 %collective-permute-start.5 = (bf16[1,4,64,256]{3,2,1,0:T(8,128)(2,1)S(1)}, bf16[1,4,64,256]{3,2,1,0:T(8,128)(2,1)S(1)}, u32[]{:S(2)}, u32[]{:S(2)}) collective-permute-start(bf16[1,4,64,256]{3,2,1,0:T(8,128)(2,1)S(1)} %shard_map.52.field), channel_id=1, source_target_pairs={{0,4},{1,5},{4,8},{5,9},{8,12},{9,13},{12,16},{13,17},{16,20},{17,... | collective-permute-start | bytes 393224 | tf_op jit(solution)/shard_map/ppermute | solution.py:51
  14.7 4.7 %collective-permute-start.4 = (bf16[1,4,64,256]{3,2,1,0:T(8,128)(2,1)S(1)}, bf16[1,4,64,256]{3,2,1,0:T(8,128)(2,1)S(1)}, u32[]{:S(2)}, u32[]{:S(2)}) collective-permute-start(bf16[1,4,64,256]{3,2,1,0:T(8,128)(2,1)S(1)} %collective-permute-done.3.odd_field), channel_id=1, source_target_pairs={{0,2},{2,0},{4,6},{6,4},{8,10},{10,8},{12,14},{14,12},{16,18},{18,... | collective-permute-start | bytes 393224 | tf_op jit(solution)/shard_map/ppermute | solution.py:55
  19.7 4.0 %collective-permute-start.6 = (bf16[1,64,256]{2,1,0:T(8,128)(2,1)S(1)}, bf16[1,64,256]{2,1,0:T(8,128)(2,1)S(1)}, u32[]{:S(2)}, u32[]{:S(2)}) collective-permute-start(bf16[1,64,256]{2,1,0:T(8,128)(2,1)S(1)} %shard_map.55), channel_id=1, source_target_pairs={{0,1},{1,0},{2,3},{3,2},{4,5},{5,4},{6,7},{7,6},{8,9},{9,8},{10,11... | collective-permute-start | bytes 98312 | tf_op jit(solution)/shard_map/ppermute | solution.py:34
where the time goes:
time: 24.5 us; the launch traced here: 24.3 us
  starting transfers between devices  9.24 us (38%)
  Pallas kernels  7.57 us (31%)
  waiting for transfers between devices  6.34 us (26%)
  local copies, waits for them, and re-layouts  1.04 us (4%)
    pallas_call x11, Pallas kernels, call(): pl.pallas_call(kernel, out_shape=out_shape, in_specs=[vmem] * (len(args)...  7.57 us
    ppermute x3, starting transfers between devices, swapped(): return lax.ppermute(value, ('tm', 'rows'), pairs)  5.12 us
    ppermute x1, starting transfers between devices, paired(): lax.ppermute(value, 'tm', [(t, t ^ 1) for t in range(lax.axis_size('tm'))])  2.8 us
    ppermute x3, waiting for transfers between devices, swapped(): return lax.ppermute(value, ('tm', 'rows'), pairs)  2.22 us
    ppermute x1, waiting for transfers between devices, ring(): return lax.ppermute(value, 'tm', [(t, (t + steps) % tm) for t in range(tm)])  2.17 us
    ppermute x1, waiting for transfers between devices, even_ahead(): lax.ppermute(value, ('tm', 'rows'), [(t * rows + r, u * rows + q) for t,...  1.94 us
    unnamed x8, local copies, waits for them, and re-layouts  1.04 us
    ppermute x1, starting transfers between devices, odd_ahead(): return lax.ppermute(value, 'tm', pairs)  0.67 us
  transfers between devices with their start and end apart: 7, of which 5 were waited for; matrix products, arithmetic and copies ran while one was open for 0% of the time, Pallas kernels for 24%

commit v1 on v0

--- a/solution.py
+++ b/solution.py
@@ -226,7 +226,8 @@
 
 
 def silu(v):
-    return v / (1.0 + jnp.exp(-v))
+    half = 0.5 * v
+    return half + half * jnp.tanh(half)
 
 
 def fine_rest_kernel(frames, weight, own, halo, out):
@@ -368,18 +369,22 @@
         ends[side] = part
 
 
-def earlier_sums(field_1, odd_field, even_field, weight, sides):
-    one = field_1[...]
-    one = jnp.where(has_earlier(1), one, jnp.zeros_like(one))
-    two = jnp.where(lax.axis_index("tm") % 2 == 1, odd_field[...], even_field[...])
-    two = jnp.where(has_earlier(2), two, jnp.zeros_like(two))
-    total_1, ends_1 = coarse_sums(one, weight, 1, sides)
-    total_2, ends_2 = coarse_sums(two, weight, 0, sides)
-    return total_1 + total_2, [x + y for x, y in zip(ends_1, ends_2)]
-
-
-def coarse_ends_kernel(field_1, odd_field, even_field, weight, ends, out):
-    _, parts = earlier_sums(field_1, odd_field, even_field, weight, ends.shape[0])
+def coarse_next_kernel(field, weight, body_in, ends_in, body, ends):
+    cells = field[...]
+    cells = jnp.where(has_earlier(1), cells, jnp.zeros_like(cells))
+    total, parts = coarse_sums(cells, weight, 1, ends.shape[0])
+    body[...] = body_in[...] + total
+    for side, part in enumerate(parts):
+        ends[side] = ends_in[side] + part
+
+
+def second_earlier(odd_field, even_field):
+    cells = jnp.where(lax.axis_index("tm") % 2 == 1, odd_field[...], even_field[...])
+    return jnp.where(has_earlier(2), cells, jnp.zeros_like(cells))
+
+
+def coarse_ends_kernel(odd_field, even_field, weight, ends, out):
+    _, parts = coarse_sums(second_earlier(odd_field, even_field), weight, 0, ends.shape[0])
     for side, part in enumerate(parts):
         out[side] = (ends[side] + part).astype(BF16)
 
@@ -388,9 +393,9 @@
     return [(rows - 1) * (1 - lax.axis_index("rows"))] if sides == 1 else [0, rows - 1]
 
 
-def coarse_body_kernel(field_1, odd_field, even_field, weight, body, out, ends, sums):
+def coarse_body_kernel(odd_field, even_field, weight, body, out, ends, sums):
     _, rows, cols, _ = out.shape
-    total, _ = earlier_sums(field_1, odd_field, even_field, weight, ends.shape[0])
+    total, _ = coarse_sums(second_earlier(odd_field, even_field), weight, 0, ends.shape[0])
     sums[...] = body[...] + total
     out[...] = silu(sums[...]).astype(BF16).reshape(out.shape)
     for side, start in enumerate(end_starts(rows, ends.shape[0])):
@@ -475,12 +480,16 @@
     body, ends = call(coarse_first_kernel, (sums, pairs), [], flops, (field, conv_coarse))
     odd_field, body, ends = lax.optimization_barrier((odd_field, body, ends))
     field_1 = paired(odd_field) if times % 2 == 0 else ring(field, 1)
+    body, ends = call(
+        coarse_next_kernel, (sums, pairs), [], flops, (field_1, conv_coarse, body, ends)
+    )
+    even_field, body, ends = lax.optimization_barrier((even_field, body, ends))
     sent = call(
         coarse_ends_kernel,
         jax.ShapeDtypeStruct(pairs.shape, BF16),
         [],
         flops // 4,
-        (field_1, odd_field, even_field, conv_coarse, ends),
+        (odd_field, even_field, conv_coarse, ends),
     )
     if sides == 1:
         added = swapped(sent, 0)
@@ -491,7 +500,7 @@
         (shape, pairs),
         [pltpu.VMEM(sums.shape, F32)],
         flops,
-        (field_1, odd_field, even_field, conv_coarse, body),
+        (odd_field, even_field, conv_coarse, body),
     )
     return call(
         finish_kernel,

time: 24.5 us -> 28.3 us (1.16)
  waiting for transfers between devices: 6.34 us -> 9.11 us
  starting transfers between devices: 9.24 us -> 10.2 us
    ppermute x1, waiting for transfers between devices: 1.94 us -> 4.36 us  [even_ahead(): lax.ppermute(value, ('tm', 'rows'), [(t * rows + r, u * rows + q) for t,...]
    ppermute x1, starting transfers between devices: 2.8 us -> 3.39 us  [paired(): lax.ppermute(value, 'tm', [(t, t ^ 1) for t in range(lax.axis_size('tm'))])]
    ppermute x3, starting transfers between devices: 5.12 us -> 5.48 us  [swapped(): return lax.ppermute(value, ('tm', 'rows'), pairs)]
    ppermute x1, waiting for transfers between devices: 0.01 us -> 0.34 us  [paired(): lax.ppermute(value, 'tm', [(t, t ^ 1) for t in range(lax.axis_size('tm'))])]
    pallas_call x11 -> x12, Pallas kernels: 7.57 us -> 7.63 us  [call(): pl.pallas_call(kernel, out_shape=out_shape, in_specs=[vmem] * (len(args)...]
  transfers between devices with their start and end apart: 7 -> 7, of which waited for: 5 -> 6; matrix products, arithmetic and copies ran while one was open for 0% -> 0% of each run, Pallas kernels for 24% -> 22%
where the time goes in v1:
time: 28.3 us; the launch traced here: 28.1 us
  starting transfers between devices  10.2 us (36%)
  waiting for transfers between devices  9.11 us (32%)
  Pallas kernels  7.63 us (27%)
  local copies, waits for them, and re-layouts  1.04 us (4%)
    pallas_call x12, Pallas kernels, call(): pl.pallas_call(kernel, out_shape=out_shape, in_specs=[vmem] * (len(args)...  7.63 us
    ppermute x3, starting transfers between devices, swapped(): return lax.ppermute(value, ('tm', 'rows'), pairs)  5.48 us
    ppermute x1, waiting for transfers between devices, even_ahead(): lax.ppermute(value, ('tm', 'rows'), [(t * rows + r, u * rows + q) for t,...  4.36 us
    ppermute x1, starting transfers between devices, paired(): lax.ppermute(value, 'tm', [(t, t ^ 1) for t in range(lax.axis_size('tm'))])  3.39 us
    ppermute x3, waiting for transfers between devices, swapped(): return lax.ppermute(value, ('tm', 'rows'), pairs)  2.24 us
    ppermute x1, waiting for transfers between devices, ring(): return lax.ppermute(value, 'tm', [(t, (t + steps) % tm) for t in range(tm)])  2.17 us
    unnamed x8, local copies, waits for them, and re-layouts  1.04 us
    ppermute x1, starting transfers between devices, odd_ahead(): return lax.ppermute(value, 'tm', pairs)  0.67 us
  transfers between devices with their start and end apart: 7, of which 6 were waited for; matrix products, arithmetic and copies ran while one was open for 0% of the time, Pallas kernels for 22%

profile of v1, /device:TPU:16, one launch (start us, length us, event | category | flops | bytes accessed | tf_op | source)
XLA Modules:
  0.0 28.1 jit_solution(5379242455512806426)
XLA Ops:
  0.0 0.0 copy-start.3
  0.0 0.0 copy-start.2
  0.0 0.0 collective-permute-start.1
  0.0 1.0 %copy-done.3 = bf16[2,8,128,128]{3,2,1,0:T(8,128)(2,1)S(1)} copy-done((bf16[2,8,128,128]{3,2,1,0:T(8,128)(2,1)S(1)}, bf16[2,8,128,128]{3,2,1,0:T(8,128)(2,1)}, u32[]{:S(2)}) %copy-start.3) | copy-done | bytes 524312
  1.1 1.6 %collective-permute-start.2 = (bf16[2,2,128,128]{3,2,1,0:T(8,128)(2,1)S(1)}, bf16[2,2,128,128]{3,2,1,0:T(8,128)(2,1)S(1)}, u32[]{:S(2)}, u32[]{:S(2)}) collective-permute-start(bf16[2,2,128,128]{3,2,1,0:T(8,128)(2,1)S(1)} %shard_map.47), channel_id=1, source_target_pairs={{0,1},{1,0},{2,3},{3,2},{4,5},{5,4},{6,7},{7,6},{8,9},{9,8},{10,11... | collective-permute-start | bytes 393224 | tf_op jit(solution)/shard_map/ppermute | solution.py:34
  2.6 2.3 %collective-permute-start = (bf16[2,2,128,128]{3,2,1,0:T(8,128)(2,1)S(1)}, bf16[2,2,128,128]{3,2,1,0:T(8,128)(2,1)S(1)}, u32[]{:S(2)}, u32[]{:S(2)}) collective-permute-start(bf16[2,2,128,128]{3,2,1,0:T(8,128)(2,1)S(1)} %shard_map.47), channel_id=1, source_target_pairs={{0,3},{1,2},{2,5},{3,4},{4,7},{5,6},{6,9},{7,8},{8,11},{9,10},{10,... | collective-permute-start | bytes 393224 | tf_op jit(solution)/shard_map/ppermute | solution.py:34
  5.0 0.0 copy-done.2
  5.0 1.5 %shard_map.48.own = f32[1152,256]{1,0:T(8,128)S(1)} custom-call(bf16[2,8,128,128]{3,2,1,0:T(8,128)(2,1)S(1)} %copy-done.3, bf16[3,3,384,128]{3,2,1,0:T(8,128)(2,1)S(1)} %copy-done.2), custom_call_target="tpu_custom_call" | custom-call | flops 1358954496 | bytes 1409024 | tf_op jit(solution)/shard_map/pallas_call | solution.py:423
  6.5 0.6 %collective-permute-done.2.above.below = bf16[2,2,128,128]{3,2,1,0:T(8,128)(2,1)S(1)} collective-permute-done((bf16[2,2,128,128]{3,2,1,0:T(8,128)(2,1)S(1)}, bf16[2,2,128,128]{3,2,1,0:T(8,128)(2,1)S(1)}, u32[]{:S(2)}, u32[]{:S(2)}) %collective-permute-start.2) | collective-permute-done | bytes 131104 | tf_op jit(solution)/shard_map/ppermute | solution.py:34
  7.1 0.4 %shard_map.49.halo = f32[384,256]{1,0:T(8,128)S(1)} custom-call(bf16[2,2,128,128]{3,2,1,0:T(8,128)(2,1)S(1)} %collective-permute-done.2.above.below, bf16[2,2,128,128]{3,2,1,0:T(8,128)(2,1)S(1)} %collective-permute-done.2.above.below, bf16[3,3,384,128]{3,2,1,0:T(8,128)(2,1)S(1)} %copy-done.2), custom_call_target="tpu_custom_call" | custom-call | flops 452984832 | bytes 1146880 | tf_op jit(solution)/shard_map/pallas_call | solution.py:423
  7.5 0.0 copy-start.1
  7.5 2.2 %collective-permute-done.1.frames = bf16[2,8,128,128]{3,2,1,0:T(8,128)(2,1)S(1)} collective-permute-done((bf16[2,8,128,128]{3,2,1,0:T(8,128)(2,1)}, bf16[2,8,128,128]{3,2,1,0:T(8,128)(2,1)S(1)}, u32[]{:S(2)}, u32[]{:S(2)}) %collective-permute-start.1) | collective-permute-done | bytes 524320 | tf_op jit(solution)/shard_map/ppermute | solution.py:28
  9.7 1.4 %shard_map.50.sums = f32[1152,256]{1,0:T(8,128)S(1)} custom-call(bf16[2,8,128,128]{3,2,1,0:T(8,128)(2,1)S(1)} %collective-permute-done.1.frames, bf16[3,3,384,128]{3,2,1,0:T(8,128)(2,1)S(1)} %copy-done.2, f32[1152,256]{1,0:T(8,128)S(1)} %shard_map.48.own, f32[384,256]{1,0:T(8,128)S(1)} %shard_map.49.halo), custom_call_target="tpu_custom_call" | custom-call | flops 1358954496 | bytes 2981888 | tf_op jit(solution)/shard_map/pallas_call | solution.py:423
  11.1 0.0 copy-done.1
  11.1 0.0 copy-start
  11.2 0.5 %shard_map.51.inner = bf16[3,64,256]{2,1,0:T(8,128)(2,1)S(1)} custom-call(f32[1152,256]{1,0:T(8,128)S(1)} %shard_map.50.sums, bf16[3,384,256]{2,1,0:T(8,128)(2,1)S(1)} %copy-done.1), custom_call_target="tpu_custom_call" | custom-call | flops 339738624 | bytes 1769472 | tf_op jit(solution)/shard_map/pallas_call | solution.py:423
  11.7 0.4 %collective-permute-done.above.below = bf16[2,2,128,128]{3,2,1,0:T(8,128)(2,1)S(1)} collective-permute-done((bf16[2,2,128,128]{3,2,1,0:T(8,128)(2,1)S(1)}, bf16[2,2,128,128]{3,2,1,0:T(8,128)(2,1)S(1)}, u32[]{:S(2)}, u32[]{:S(2)}) %collective-permute-start) | collective-permute-done | bytes 131104 | tf_op jit(solution)/shard_map/ppermute | solution.py:34
  12.1 0.7 %shard_map.52.field = bf16[1,4,64,256]{3,2,1,0:T(8,128)(2,1)S(1)} custom-call(bf16[2,2,128,128]{3,2,1,0:T(8,128)(2,1)S(1)} %collective-permute-done.above.below, bf16[2,2,128,128]{3,2,1,0:T(8,128)(2,1)S(1)} %collective-permute-done.above.below, bf16[3,3,384,128]{3,2,1,0:T(8,128)(2,1)S(1)} %copy-done.2, f32[1152,256]{1,0:T(8,128)S(1)} %shard_map.50.sums, ...), custom_call_target="tpu_custom_call" | custom-call | flops 452984832 | bytes 3014656 | tf_op jit(solution)/shard_map/pallas_call | solution.py:423
  12.8 0.7 %collective-permute-start.3 = (bf16[1,4,64,256]{3,2,1,0:T(8,128)(2,1)S(1)}, bf16[1,4,64,256]{3,2,1,0:T(8,128)(2,1)S(1)}, u32[]{:S(2)}, u32[]{:S(2)}) collective-permute-start(bf16[1,4,64,256]{3,2,1,0:T(8,128)(2,1)S(1)} %shard_map.52.field), channel_id=1, source_target_pairs={{2,6},{6,10},{10,14},{14,18},{18,22},{22,26},{26,30},{0,0},{4,4},{... | collective-permute-start | bytes 393224 | tf_op jit(solution)/shard_map/ppermute | solution.py:40
  13.5 0.0 copy-done
  13.5 0.5 %shard_map.53 = (f32[256,256]{1,0:T(8,128)S(1)}, f32[1,64,256]{2,1,0:T(8,128)S(1)}) custom-call(bf16[1,4,64,256]{3,2,1,0:T(8,128)(2,1)S(1)} %shard_map.52.field, bf16[3,3,768,256]{3,2,1,0:T(8,128)(2,1)S(1)} %copy-done), custom_call_target="tpu_custom_call" | custom-call | flops 301989888 | bytes 3670016 | tf_op jit(solution)/shard_map/pallas_call | solution.py:423
  14.0 0.0 collective-permute-done.3.odd_field
  14.0 3.4 %collective-permute-start.5 = (bf16[1,4,64,256]{3,2,1,0:T(8,128)(2,1)S(1)}, bf16[1,4,64,256]{3,2,1,0:T(8,128)(2,1)S(1)}, u32[]{:S(2)}, u32[]{:S(2)}) collective-permute-start(bf16[1,4,64,256]{3,2,1,0:T(8,128)(2,1)S(1)} %collective-permute-done.3.odd_field), channel_id=1, source_target_pairs={{0,2},{2,0},{4,6},{6,4},{8,10},{10,8},{12,14},{14,12},{16,18},{18,... | collective-permute-start | bytes 393224 | tf_op jit(solution)/shard_map/ppermute | solution.py:55
  17.4 0.6 %collective-permute-start.4 = (bf16[1,4,64,256]{3,2,1,0:T(8,128)(2,1)S(1)}, bf16[1,4,64,256]{3,2,1,0:T(8,128)(2,1)S(1)}, u32[]{:S(2)}, u32[]{:S(2)}) collective-permute-start(bf16[1,4,64,256]{3,2,1,0:T(8,128)(2,1)S(1)} %shard_map.52.field), channel_id=1, source_target_pairs={{0,4},{1,5},{4,8},{5,9},{8,12},{9,13},{12,16},{13,17},{16,20},{17,... | collective-permute-start | bytes 393224 | tf_op jit(solution)/shard_map/ppermute | solution.py:51
  18.1 0.3 %collective-permute-done.5.field = bf16[1,4,64,256]{3,2,1,0:T(8,128)(2,1)S(1)} collective-permute-done((bf16[1,4,64,256]{3,2,1,0:T(8,128)(2,1)S(1)}, bf16[1,4,64,256]{3,2,1,0:T(8,128)(2,1)S(1)}, u32[]{:S(2)}, u32[]{:S(2)}) %collective-permute-start.5) | collective-permute-done | bytes 131104 | tf_op jit(solution)/shard_map/ppermute | solution.py:55
  18.4 0.5 %shard_map.54 = (f32[256,256]{1,0:T(8,128)S(1)}, f32[1,64,256]{2,1,0:T(8,128)S(1)}) custom-call(bf16[1,4,64,256]{3,2,1,0:T(8,128)(2,1)S(1)} %collective-permute-done.5.field, bf16[3,3,768,256]{3,2,1,0:T(8,128)(2,1)S(1)} %copy-done, f32[256,256]{1,0:T(8,128)S(1)} %get-tuple-element.28.body_in, f32[1,64,256]{2,1,0:T(8,128)S(1)} %get-tuple-element.29.ends_in), custom_call_target="tpu_custom_call" | custom-call | flops 301989888 | bytes 3997696 | tf_op jit(solution)/shard_map/pallas_call | solution.py:423
  18.9 4.4 %collective-permute-done.4.even_field = bf16[1,4,64,256]{3,2,1,0:T(8,128)(2,1)S(1)} collective-permute-done((bf16[1,4,64,256]{3,2,1,0:T(8,128)(2,1)S(1)}, bf16[1,4,64,256]{3,2,1,0:T(8,128)(2,1)S(1)}, u32[]{:S(2)}, u32[]{:S(2)}) %collective-permute-start.4) | collective-permute-done | bytes 131104 | tf_op jit(solution)/shard_map/ppermute | solution.py:51
  23.3 0.2 shard_map.56
  23.5 1.6 %collective-permute-start.6 = (bf16[1,64,256]{2,1,0:T(8,128)(2,1)S(1)}, bf16[1,64,256]{2,1,0:T(8,128)(2,1)S(1)}, u32[]{:S(2)}, u32[]{:S(2)}) collective-permute-start(bf16[1,64,256]{2,1,0:T(8,128)(2,1)S(1)} %shard_map.56), channel_id=1, source_target_pairs={{0,1},{1,0},{2,3},{3,2},{4,5},{5,4},{6,7},{7,6},{8,9},{9,8},{10,11... | collective-permute-start | bytes 98312 | tf_op jit(solution)/shard_map/ppermute | solution.py:34
  25.1 1.2 %shard_map.55 = (bf16[1,4,64,256]{3,2,1,0:T(8,128)(2,1)}, f32[1,64,256]{2,1,0:T(8,128)S(1)}) custom-call(bf16[1,4,64,256]{3,2,1,0:T(8,128)(2,1)S(1)} %collective-permute-done.3.odd_field, bf16[1,4,64,256]{3,2,1,0:T(8,128)(2,1)S(1)} %collective-permute-done.4.even_field, bf16[3,3,768,256]{3,2,1,0:T(8,128)(2,1)S(1)} %copy-done, ...), custom_call_target="tpu_custom_call" | custom-call | flops 301989888 | bytes 4063232 | tf_op jit(solution)/shard_map/pallas_call | solution.py:423
  26.2 1.2 %collective-permute-done.6.added = bf16[1,64,256]{2,1,0:T(8,128)(2,1)S(1)} collective-permute-done((bf16[1,64,256]{2,1,0:T(8,128)(2,1)S(1)}, bf16[1,64,256]{2,1,0:T(8,128)(2,1)S(1)}, u32[]{:S(2)}, u32[]{:S(2)}) %collective-permute-start.6) | collective-permute-done | bytes 32800 | tf_op jit(solution)/shard_map/ppermute | solution.py:34
  27.5 0.6 %shard_map.57 = bf16[1,4,64,256]{3,2,1,0:T(8,128)(2,1)} custom-call(f32[1,64,256]{2,1,0:T(8,128)S(1)} %get-tuple-element.34.ends, bf16[1,64,256]{2,1,0:T(8,128)(2,1)S(1)} %collective-permute-done.6.added, bf16[1,4,64,256]{3,2,1,0:T(8,128)(2,1)} %get-tuple-element.36._), custom_call_target="tpu_custom_call", output_to_operand_aliasing={{}: (2, {})} | custom-call | flops 18874368 | bytes 229376 | tf_op jit(solution)/shard_map/pallas_call | solution.py:423
  (2 shorter events, 0.0 us)
Async XLA Ops:
  0.0 1.0 %copy-start.3 = (bf16[2,8,128,128]{3,2,1,0:T(8,128)(2,1)S(1)}, bf16[2,8,128,128]{3,2,1,0:T(8,128)(2,1)}, u32[]{:S(2)}) copy-start(bf16[2,8,128,128]{3,2,1,0:T(8,128)(2,1)} %frames.1) | copy-start | bytes 1572868
  0.0 4.9 %copy-start.2 = (bf16[3,3,384,128]{3,2,1,0:T(8,128)(2,1)S(1)}, bf16[3,3,384,128]{3,2,1,0:T(8,128)(2,1)}, u32[]{:S(2)}) copy-start(bf16[3,3,384,128]{3,2,1,0:T(8,128)(2,1)} %weight.11) | copy-start | bytes 2654212
  0.0 9.7 %collective-permute-start.1 = (bf16[2,8,128,128]{3,2,1,0:T(8,128)(2,1)}, bf16[2,8,128,128]{3,2,1,0:T(8,128)(2,1)S(1)}, u32[]{:S(2)}, u32[]{:S(2)}) collective-permute-start(bf16[2,8,128,128]{3,2,1,0:T(8,128)(2,1)} %frames.1), channel_id=1, source_target_pairs={{0,2},{2,4},{4,6},{6,8},{8,10},{10,12},{12,14},{14,16},{16,18},{18... | collective-permute-start | bytes 1572872 | tf_op jit(solution)/shard_map/ppermute | solution.py:28
  1.1 6.0 %collective-permute-start.2 = (bf16[2,2,128,128]{3,2,1,0:T(8,128)(2,1)S(1)}, bf16[2,2,128,128]{3,2,1,0:T(8,128)(2,1)S(1)}, u32[]{:S(2)}, u32[]{:S(2)}) collective-permute-start(bf16[2,2,128,128]{3,2,1,0:T(8,128)(2,1)S(1)} %shard_map.47), channel_id=1, source_target_pairs={{0,1},{1,0},{2,3},{3,2},{4,5},{5,4},{6,7},{7,6},{8,9},{9,8},{10,11... | collective-permute-start | bytes 393224 | tf_op jit(solution)/shard_map/ppermute | solution.py:34
  2.6 9.4 %collective-permute-start = (bf16[2,2,128,128]{3,2,1,0:T(8,128)(2,1)S(1)}, bf16[2,2,128,128]{3,2,1,0:T(8,128)(2,1)S(1)}, u32[]{:S(2)}, u32[]{:S(2)}) collective-permute-start(bf16[2,2,128,128]{3,2,1,0:T(8,128)(2,1)S(1)} %shard_map.47), channel_id=1, source_target_pairs={{0,3},{1,2},{2,5},{3,4},{4,7},{5,6},{6,9},{7,8},{8,11},{9,10},{10,... | collective-permute-start | bytes 393224 | tf_op jit(solution)/shard_map/ppermute | solution.py:34
  7.5 3.6 %copy-start.1 = (bf16[3,384,256]{2,1,0:T(8,128)(2,1)S(1)}, bf16[3,384,256]{2,1,0:T(8,128)(2,1)}, u32[]{:S(2)}) copy-start(bf16[3,384,256]{2,1,0:T(8,128)(2,1)} %down.3) | copy-start | bytes 1769476
  11.1 2.3 %copy-start = (bf16[3,3,768,256]{3,2,1,0:T(8,128)(2,1)S(1)}, bf16[3,3,768,256]{3,2,1,0:T(8,128)(2,1)}, u32[]{:S(2)}) copy-start(bf16[3,3,768,256]{3,2,1,0:T(8,128)(2,1)} %weight.15) | copy-start | bytes 10616836
  12.8 1.2 %collective-permute-start.3 = (bf16[1,4,64,256]{3,2,1,0:T(8,128)(2,1)S(1)}, bf16[1,4,64,256]{3,2,1,0:T(8,128)(2,1)S(1)}, u32[]{:S(2)}, u32[]{:S(2)}) collective-permute-start(bf16[1,4,64,256]{3,2,1,0:T(8,128)(2,1)S(1)} %shard_map.52.field), channel_id=1, source_target_pairs={{2,6},{6,10},{10,14},{14,18},{18,22},{22,26},{26,30},{0,0},{4,4},{... | collective-permute-start | bytes 393224 | tf_op jit(solution)/shard_map/ppermute | solution.py:40
  14.0 4.4 %collective-permute-start.5 = (bf16[1,4,64,256]{3,2,1,0:T(8,128)(2,1)S(1)}, bf16[1,4,64,256]{3,2,1,0:T(8,128)(2,1)S(1)}, u32[]{:S(2)}, u32[]{:S(2)}) collective-permute-start(bf16[1,4,64,256]{3,2,1,0:T(8,128)(2,1)S(1)} %collective-permute-done.3.odd_field), channel_id=1, source_target_pairs={{0,2},{2,0},{4,6},{6,4},{8,10},{10,8},{12,14},{14,12},{16,18},{18,... | collective-permute-start | bytes 393224 | tf_op jit(solution)/shard_map/ppermute | solution.py:55
  17.4 5.9 %collective-permute-start.4 = (bf16[1,4,64,256]{3,2,1,0:T(8,128)(2,1)S(1)}, bf16[1,4,64,256]{3,2,1,0:T(8,128)(2,1)S(1)}, u32[]{:S(2)}, u32[]{:S(2)}) collective-permute-start(bf16[1,4,64,256]{3,2,1,0:T(8,128)(2,1)S(1)} %shard_map.52.field), channel_id=1, source_target_pairs={{0,4},{1,5},{4,8},{5,9},{8,12},{9,13},{12,16},{13,17},{16,20},{17,... | collective-permute-start | bytes 393224 | tf_op jit(solution)/shard_map/ppermute | solution.py:51
  23.5 4.0 %collective-permute-start.6 = (bf16[1,64,256]{2,1,0:T(8,128)(2,1)S(1)}, bf16[1,64,256]{2,1,0:T(8,128)(2,1)S(1)}, u32[]{:S(2)}, u32[]{:S(2)}) collective-permute-start(bf16[1,64,256]{2,1,0:T(8,128)(2,1)S(1)} %shard_map.56), channel_id=1, source_target_pairs={{0,1},{1,0},{2,3},{3,2},{4,5},{5,4},{6,7},{7,6},{8,9},{9,8},{10,11... | collective-permute-start | bytes 98312 | tf_op jit(solution)/shard_map/ppermute | solution.py:34
